TPU v7x, 512 devices: a whole 4x4x16 slice. The times are simulated.
512 devices in a mesh: gx: 16 (over z), gy: 4 (over x), gz: 8 (over y, core).
Axes of the slice: x: 4, y: 4, z: 16, core: 2. Of those that a mesh axis runs over, the one named last changes fastest.
Arguments:
- flow: float32 [4, 128, 64, 1024], P(None, 'gx', 'gy', 'gz'), may hold values from -3 to 3
- basis: float32 [127, 3, 131072], P(None, None, ('gx', 'gy', 'gz')), may hold values from -1150 to 1150
- sample: int32 [131072], P(('gx', 'gy', 'gz')), may hold values from 0 to 16383
Outputs:
- flow_next: float32 [4, 128, 64, 1024], P(None, 'gx', 'gy', 'gz')
- basis_next: float32 [128, 3, 131072], P(None, None, ('gx', 'gy', 'gz'))
- factor: float32 [128, 128], replicated
All inputs are finite; a program needn't handle non-finite values.
Results may differ from a plain program's by a relative error of at most 0.000065.
Values sent between devices are 32-bit elements; how exact they have to be, the bound alone decides.
A program may use at most 64 MiB of HBM per device.

v0:
```python
import jax
import jax.numpy as jnp
from jax import lax
from jax.sharding import PartitionSpec as P

DT_STEP = 0.35
VISCOSITY = 0.2
SOUND_SQ = 1.0
DRIVING = 0.5


def padded(block, sides, width, periodic):
    for axis, dim in sides:
        count = lax.axis_size(axis)
        forward = [(i, i + 1) for i in range(count - 1)]
        if periodic:
            forward.append((count - 1, 0))
        backward = [(target, source) for source, target in forward]
        low = lax.ppermute(
            lax.slice_in_dim(block, block.shape[dim] - width, None, axis=dim), axis, forward
        )
        high = lax.ppermute(lax.slice_in_dim(block, 0, width, axis=dim), axis, backward)
        block = jnp.concatenate([low, block, high], axis=dim)
    return block


def rates(ext):
    centre = ext[:, 1:-1, 1:-1, 1:-1]
    x_plus = ext[:, 2:, 1:-1, 1:-1]
    x_minus = ext[:, :-2, 1:-1, 1:-1]
    y_plus = ext[:, 1:-1, 2:, 1:-1]
    y_minus = ext[:, 1:-1, :-2, 1:-1]
    z_plus = ext[:, 1:-1, 1:-1, 2:]
    z_minus = ext[:, 1:-1, 1:-1, :-2]
    slope_x = 0.5 * (x_plus - x_minus)
    slope_y = 0.5 * (y_plus - y_minus)
    slope_z = 0.5 * (z_plus - z_minus)
    laplace = x_plus + x_minus + (y_plus + y_minus) + (z_plus + z_minus) - 6.0 * centre
    advect = centre[0] * slope_x[:3] + centre[1] * slope_y[:3] + centre[2] * slope_z[:3]
    pressure = jnp.stack([slope_x[3], slope_y[3], slope_z[3]])
    forcing = jnp.array([DRIVING, 0.0, 0.0], dtype=jnp.float32).reshape(3, 1, 1, 1)
    velocity = VISCOSITY * laplace[:3] - advect - pressure + forcing
    density = -SOUND_SQ * (slope_x[0] + slope_y[1] + slope_z[2])
    return jnp.concatenate([velocity, density[None]], axis=0)


def extend_one(fields):
    walled = padded(fields, (("gy", 2),), 1, False)
    return padded(walled, (("gx", 1), ("gz", 3)), 1, True)


def local(flow, basis, sample):
    points = basis.shape[2]
    modes = basis.shape[0]
    count = 3.0 * points * lax.axis_size("gx") * lax.axis_size("gy") * lax.axis_size("gz")
    section_one = flow + DT_STEP * rates(extend_one(flow))
    section_two = 0.75 * flow + 0.25 * (section_one + DT_STEP * rates(extend_one(section_one)))
    flow_next = 1.0 / 3.0 * flow + 2.0 / 3.0 * (
        section_two + DT_STEP * rates(extend_one(section_two))
    )
    velocity = flow_next[:3].reshape(3, -1)
    snapshot = jnp.take(velocity, sample, axis=1)
    stacked = jnp.concatenate([basis, snapshot[None]], axis=0).reshape(modes + 1, 3 * points)
    local_gram = jnp.dot(
        stacked, stacked.T, precision=lax.Precision.HIGHEST, preferred_element_type=jnp.float32
    )
    gram = lax.psum(local_gram, ("gx", "gy", "gz")) / count
    lower = jnp.linalg.cholesky(gram)
    basis_next = jax.scipy.linalg.solve_triangular(lower, stacked, lower=True).reshape(
        modes + 1, 3, points
    )
    return (flow_next, basis_next, lower.T)


def solution(mesh):
    return jax.shard_map(
        local,
        mesh=mesh,
        in_specs=(
            P(None, "gx", "gy", "gz"),
            P(None, None, ("gx", "gy", "gz")),
            P(("gx", "gy", "gz")),
        ),
        out_specs=(P(None, "gx", "gy", "gz"), P(None, None, ("gx", "gy", "gz")), P()),
        check_vma=False,
    )
```

profile of v0, /device:TPU:1, one launch (start us, length us, event | category | flops | bytes accessed | tf_op | source)
XLA Modules:
  0.0 582.4 jit_solution(7620865436270588193)
XLA Ops:
  7.2 1.0 fusion.68
  8.3 3.9 collective-permute-start
  12.2 1.3 collective-permute-start.1
  13.5 0.9 slice_bitcast_fusion.8
  14.4 2.2 collective-permute-done.1
  16.7 0.8 pad_maximum_fusion.64
  17.5 11.1 %collective-permute-start.2 = (f32[4,1,18,128]{3,2,1,0:T(8,128)S(1)}, f32[4,1,18,128]{3,2,1,0:T(8,128)S(1)}, u32[]{:S(2)}, u32[]{:S(2)}) collective-permute-start(f32[4,1,18,128]{3,2,1,0:T(8,128)S(1)} %get-tuple-element.41), channel_id=1, source_target_pairs={{32,0},{64,32},{96,64},{128,96},{160,128},{192,160},{224,192},{256... | collective-permute-start | bytes 110600 | tf_op jit(solution)/shard_map/ppermute | solution.py:22
  28.6 1.9 collective-permute-start.3
  30.6 0.7 compare_select_fusion
  31.2 3.4 collective-permute-done.3
  34.7 1.0 pad_maximum_fusion
  35.9 3.5 collective-permute-start.4
  39.4 1.2 collective-permute-start.5
  40.6 1.6 subtract_multiply_fusion.5
  42.2 5.2 collective-permute-done.4
  47.4 1.4 subtract_multiply_fusion.4
  48.9 1.5 fusion.24
  50.4 3.1 collective-permute-start.6
  53.6 1.3 collective-permute-start.7
  54.9 3.1 collective-permute-done.7
  58.1 1.9 collective-permute-start.8
  60.0 3.4 collective-permute-start.9
  63.4 2.6 collective-permute-done.9
  66.3 4.2 collective-permute-start.10
  70.7 6.5 %collective-permute-done.10 = f32[4,10,18,1]{3,2,1,0:T(8,128)S(1)} collective-permute-done((f32[4,10,18,1]{3,2,1,0:T(8,128)S(1)}, f32[4,10,18,1]{3,2,1,0:T(8,128)S(1)}, u32[]{:S(2)}, u32[]{:S(2)}) %collective-permute-start.10) | collective-permute-done | bytes 2912 | tf_op jit(solution)/shard_map/ppermute | solution.py:22
  77.2 0.3 subtract_multiply_fusion.2
  77.9 2.8 collective-permute-start.12
  80.7 1.3 collective-permute-start.13
  82.2 3.0 collective-permute-done.13
  85.2 1.9 collective-permute-start.14
  87.1 3.5 collective-permute-start.15
  90.7 2.5 collective-permute-done.15
  93.4 5.4 collective-permute-start.16
  99.0 5.4 collective-permute-done.16
  104.5 0.2 collective-permute-done.17
  104.7 0.3 subtract_multiply_fusion
  105.3 4.7 copy.16
  110.1 4.1 gather_fusion
  114.3 1.1 convolution_bitcast_fusion
  115.8 433.0 %all-reduce.2.cloned.1.call-done = f32[128,128]{0,1:T(8,128)} async-done(((f32[128,128]{0,1:T(8,128)}), f32[128,128]{0,1:T(8,128)}) %all-reduce.2.cloned.1.call-update) | async-done | bytes 65552 | tf_op jit(solution)/shard_map/psum | solution.py:67
  548.8 0.8 broadcast_multiply_fusion
  549.8 0.9 fusion.57
  550.6 11.7 %cholesky.16 = f32[128,128]{1,0:T(8,128)S(1)} custom-call(f32[128,128]{1,0:T(8,128)S(1)} %fusion.57), custom_call_target="Cholesky" | custom-call | tf_op jit(solution)/shard_map/jit(cholesky)/cholesky | solution.py:68
  562.4 0.6 compare_reduce_fusion
  563.0 0.7 fusion.58
  563.7 9.8 %custom-call.7 = f32[1,128,128]{1,2,0:T(8,128)S(1)} custom-call(f32[1,128,128]{2,1,0:T(8,128)S(1)} %get-tuple-element.70), custom_call_target="InvertDiagBlocksLowerTriangular" | custom-call | tf_op jit(solution)/shard_map/jit(_solve_triangular)/triangular_solve | solution.py:69
  573.5 0.7 copy.23
  574.2 1.3 fusion.55
  (55 shorter events, 2.6 us)
Async XLA Ops:
  7.2 43.2 %copy-start = (f32[4,8,16,128]{3,2,1,0:T(8,128)S(1)}, f32[4,8,16,128]{3,2,1,0:T(8,128)}, u32[]{:S(2)}) copy-start(f32[4,8,16,128]{3,2,1,0:T(8,128)} %param.6) | copy-start | bytes 786436
  7.2 47.7 %copy-start.4 = (s32[256]{0:T(256)S(1)}, s32[256]{0:T(256)}, u32[]{:S(2)}) copy-start(s32[256]{0:T(256)} %param.8) | copy-start | bytes 3076
  7.2 541.6 %all-reduce.2.cloned.1.call-start = ((), (), s32[]{:S(2)}) async-start(), calls=%async_computation | async-start | bytes 131072 | tf_op jit(solution)/shard_map/psum | solution.py:67
  8.3 6.2 %collective-permute-start = (f32[4,8,1,128]{3,2,1,0:T(1,128)S(1)}, f32[4,8,1,128]{3,2,1,0:T(1,128)S(1)}, u32[]{:S(2)}, u32[]{:S(2)}) collective-permute-start(f32[4,8,1,128]{3,2,1,0:T(1,128)S(1)} %get-tuple-element.67), channel_id=1, source_target_pairs={{0,8},{8,16},{16,24},{1,9},{9,17},{17,25},{2,10},{10,18},{18,26},{... | collective-permute-start | bytes 49160 | tf_op jit(solution)/shard_map/ppermute | solution.py:19
  12.2 4.5 collective-permute-start.1
  17.5 13.7 %collective-permute-start.2 = (f32[4,1,18,128]{3,2,1,0:T(8,128)S(1)}, f32[4,1,18,128]{3,2,1,0:T(8,128)S(1)}, u32[]{:S(2)}, u32[]{:S(2)}) collective-permute-start(f32[4,1,18,128]{3,2,1,0:T(8,128)S(1)} %get-tuple-element.41), channel_id=1, source_target_pairs={{32,0},{64,32},{96,64},{128,96},{160,128},{192,160},{224,192},{256... | collective-permute-start | bytes 110600 | tf_op jit(solution)/shard_map/ppermute | solution.py:22
  28.6 6.0 %collective-permute-start.3 = (f32[4,1,18,128]{3,2,1,0:T(8,128)S(1)}, f32[4,1,18,128]{3,2,1,0:T(8,128)S(1)}, u32[]{:S(2)}, u32[]{:S(2)}) collective-permute-start(f32[4,1,18,128]{3,2,1,0:T(8,128)S(1)} %get-tuple-element.40), channel_id=1, source_target_pairs={{0,32},{32,64},{64,96},{96,128},{128,160},{160,192},{192,224},{224... | collective-permute-start | bytes 110600 | tf_op jit(solution)/shard_map/ppermute | solution.py:19
  35.7 41.9 %copy-start.3 = (f32[3]{0:T(128)S(1)}, f32[3]{0:T(128)}, u32[]{:S(2)}) copy-start(f32[3]{0:T(128)} %constant.80.clone) | copy-start | bytes 40
  35.9 11.5 %collective-permute-start.4 = (f32[4,10,18,1]{3,2,1,0:T(8,128)S(1)}, f32[4,10,18,1]{3,2,1,0:T(8,128)S(1)}, u32[]{:S(2)}, u32[]{:S(2)}) collective-permute-start(f32[4,10,18,1]{3,2,1,0:T(8,128)S(1)} %get-tuple-element.31), channel_id=1, source_target_pairs={{1,0},{2,1},{3,2},{4,3},{5,4},{6,5},{7,6},{0,7},{9,8},{10,9},{11,1... | collective-permute-start | bytes 8648 | tf_op jit(solution)/shard_map/ppermute | solution.py:22
  39.4 8.0 %collective-permute-start.5 = (f32[4,10,18,1]{3,2,1,0:T(8,128)S(1)}, f32[4,10,18,1]{3,2,1,0:T(8,128)S(1)}, u32[]{:S(2)}, u32[]{:S(2)}) collective-permute-start(f32[4,10,18,1]{3,2,1,0:T(8,128)S(1)} %get-tuple-element.32), channel_id=1, source_target_pairs={{0,1},{1,2},{2,3},{3,4},{4,5},{5,6},{6,7},{7,0},{8,9},{9,10},{10,1... | collective-permute-start | bytes 8648 | tf_op jit(solution)/shard_map/ppermute | solution.py:19
  42.2 39.8 %copy-start.1 = (f32[127,3,256]{2,0,1:T(8,128)S(1)}, f32[127,3,256]{2,0,1:T(8,128)}, u32[]{:S(2)}) copy-start(f32[127,3,256]{2,0,1:T(8,128)} %param.7) | copy-start | bytes 1170436
  50.4 4.5 collective-permute-start.6
  53.6 4.5 collective-permute-start.7
  58.1 5.3 collective-permute-start.8
  60.0 6.0 %collective-permute-start.9 = (f32[4,1,18,128]{3,2,1,0:T(8,128)S(1)}, f32[4,1,18,128]{3,2,1,0:T(8,128)S(1)}, u32[]{:S(2)}, u32[]{:S(2)}) collective-permute-start(f32[4,1,18,128]{3,2,1,0:T(8,128)S(1)} %get-tuple-element.37), channel_id=1, source_target_pairs={{0,32},{32,64},{64,96},{96,128},{128,160},{160,192},{192,224},{224... | collective-permute-start | bytes 110600 | tf_op jit(solution)/shard_map/ppermute | solution.py:19
  66.3 10.9 %collective-permute-start.10 = (f32[4,10,18,1]{3,2,1,0:T(8,128)S(1)}, f32[4,10,18,1]{3,2,1,0:T(8,128)S(1)}, u32[]{:S(2)}, u32[]{:S(2)}) collective-permute-start(f32[4,10,18,1]{3,2,1,0:T(8,128)S(1)} %get-tuple-element.29), channel_id=1, source_target_pairs={{1,0},{2,1},{3,2},{4,3},{5,4},{6,5},{7,6},{0,7},{9,8},{10,9},{11,1... | collective-permute-start | bytes 8648 | tf_op jit(solution)/shard_map/ppermute | solution.py:22
  70.5 6.6 %collective-permute-start.11 = (f32[4,10,18,1]{3,2,1,0:T(8,128)S(1)}, f32[4,10,18,1]{3,2,1,0:T(8,128)S(1)}, u32[]{:S(2)}, u32[]{:S(2)}) collective-permute-start(f32[4,10,18,1]{3,2,1,0:T(8,128)S(1)} %get-tuple-element.30), channel_id=1, source_target_pairs={{0,1},{1,2},{2,3},{3,4},{4,5},{5,6},{6,7},{7,0},{8,9},{9,10},{10,1... | collective-permute-start | bytes 8648 | tf_op jit(solution)/shard_map/ppermute | solution.py:19
  77.9 4.3 collective-permute-start.12
  80.7 4.5 collective-permute-start.13
  85.2 5.5 collective-permute-start.14
  87.1 6.0 %collective-permute-start.15 = (f32[4,1,18,128]{3,2,1,0:T(8,128)S(1)}, f32[4,1,18,128]{3,2,1,0:T(8,128)S(1)}, u32[]{:S(2)}, u32[]{:S(2)}) collective-permute-start(f32[4,1,18,128]{3,2,1,0:T(8,128)S(1)} %get-tuple-element.34), channel_id=1, source_target_pairs={{0,32},{32,64},{64,96},{96,128},{128,160},{160,192},{192,224},{224... | collective-permute-start | bytes 110600 | tf_op jit(solution)/shard_map/ppermute | solution.py:19
  93.4 11.0 %collective-permute-start.16 = (f32[4,10,18,1]{3,2,1,0:T(8,128)S(1)}, f32[4,10,18,1]{3,2,1,0:T(8,128)S(1)}, u32[]{:S(2)}, u32[]{:S(2)}) collective-permute-start(f32[4,10,18,1]{3,2,1,0:T(8,128)S(1)} %get-tuple-element.27), channel_id=1, source_target_pairs={{1,0},{2,1},{3,2},{4,3},{5,4},{6,5},{7,6},{0,7},{9,8},{10,9},{11,1... | collective-permute-start | bytes 8648 | tf_op jit(solution)/shard_map/ppermute | solution.py:22
  98.9 5.8 collective-permute-start.17
  105.3 470.2 %copy-start.2 = (f32[4,8,16,128]{3,2,1,0:T(8,128)}, f32[4,8,16,128]{3,2,1,0:T(8,128)S(1)}, u32[]{:S(2)}) copy-start(f32[4,8,16,128]{3,2,1,0:T(8,128)S(1)} %fusion.15) | copy-start | bytes 786436
Sparse Core Ops, SparseCore 0:
  115.5 433.2 all-reduce.1
where the time goes:
time: 583 us; the launch traced here: 582 us
  waiting for transfers between devices  467 us (80%)
  starting transfers between devices  52 us (9%)
  other arithmetic  33.4 us (6%)
  between operations  14.5 us (2%)
  local copies, waits for them, and re-layouts  12.7 us (2%)
    psum x1, waiting for transfers between devices, local(): gram = lax.psum(local_gram, ('gx', 'gy', 'gz')) / count  433 us
    ppermute x9, starting transfers between devices, padded(): lax.ppermute(lax.slice_in_dim(block, 0, width, axis=dim), axis, backward)  32.1 us
    ppermute x9, waiting for transfers between devices, padded(): lax.ppermute(lax.slice_in_dim(block, 0, width, axis=dim), axis, backward)  25.5 us
    ppermute x9, starting transfers between devices, padded(): lax.ppermute(lax.slice_in_dim(block, block.shape[dim] - width, None, axis...  19.9 us
    another operation x3, other arithmetic, local(): lower = jnp.linalg.cholesky(gram)  12.4 us
  transfers between devices with their start and end apart: 19, of which 11 were waited for; matrix products, arithmetic and copies ran while one was open for 1% of the time, Pallas kernels for 0%

commit v1 on v0

--- a/solution.py
+++ b/solution.py
@@ -64,7 +64,7 @@
     local_gram = jnp.dot(
         stacked, stacked.T, precision=lax.Precision.HIGHEST, preferred_element_type=jnp.float32
     )
-    gram = lax.psum(local_gram, ("gx", "gy", "gz")) / count
+    gram = jnp.sum(lax.all_gather(local_gram, ("gx", "gy", "gz")), axis=0) / count
     lower = jnp.linalg.cholesky(gram)
     basis_next = jax.scipy.linalg.solve_triangular(lower, stacked, lower=True).reshape(
         modes + 1, 3, points

time: 583 us -> 393 us (0.67)
  waiting for transfers between devices: 467 us -> 265 us
  other arithmetic: 33.4 us -> 44.8 us
    psum x1 -> x0, waiting for transfers between devices: 433 us -> none  [local(): gram = lax.psum(local_gram, ('gx', 'gy', 'gz')) / count]
    all_gather x0 -> x1, waiting for transfers between devices: none -> 231 us  [local(): lax.all_gather(local_gram, ('gx', 'gy', 'gz'))]
    reduce_sum x0 -> x1, other arithmetic: none -> 13.1 us  [local(): jnp.sum(lax.all_gather(local_gram, ('gx', 'gy', 'gz')), axis=0) / count]
where the time goes in v1:
time: 393 us; the launch traced here: 392 us
  waiting for transfers between devices  265 us (67%)
  starting transfers between devices  52 us (13%)
  other arithmetic  44.8 us (11%)
  between operations  14.5 us (4%)
  local copies, waits for them, and re-layouts  12.8 us (3%)
    all_gather x1, waiting for transfers between devices, local(): lax.all_gather(local_gram, ('gx', 'gy', 'gz'))  231 us
    ppermute x9, starting transfers between devices, padded(): lax.ppermute(lax.slice_in_dim(block, 0, width, axis=dim), axis, backward)  32.1 us
    ppermute x9, waiting for transfers between devices, padded(): lax.ppermute(lax.slice_in_dim(block, 0, width, axis=dim), axis, backward)  25.7 us
    ppermute x9, starting transfers between devices, padded(): lax.ppermute(lax.slice_in_dim(block, block.shape[dim] - width, None, axis...  19.9 us
    reduce_sum x1, other arithmetic, local(): jnp.sum(lax.all_gather(local_gram, ('gx', 'gy', 'gz')), axis=0) / count  13.1 us
    another operation x3, other arithmetic, local(): lower = jnp.linalg.cholesky(gram)  12.4 us
    another operation x1, other arithmetic, local(): jax.scipy.linalg.solve_triangular(lower, stacked, lower=True)  9.81 us
    ppermute x9, waiting for transfers between devices, padded(): lax.ppermute(lax.slice_in_dim(block, block.shape[dim] - width, None, axis...  8.75 us
  transfers between devices with their start and end apart: 19, of which 11 were waited for; matrix products, arithmetic and copies ran while one was open for 1% of the time, Pallas kernels for 0%

profile of v1, /device:TPU:1, one launch (start us, length us, event | category | flops | bytes accessed | tf_op | source)
XLA Modules:
  0.0 392.0 jit_solution(13465562421725911790)
XLA Ops:
  7.2 1.0 fusion.68
  8.3 3.9 %collective-permute-start = (f32[4,8,1,128]{3,2,1,0:T(1,128)S(1)}, f32[4,8,1,128]{3,2,1,0:T(1,128)S(1)}, u32[]{:S(2)}, u32[]{:S(2)}) collective-permute-start(f32[4,8,1,128]{3,2,1,0:T(1,128)S(1)} %get-tuple-element.70), channel_id=1, source_target_pairs={{0,8},{8,16},{16,24},{1,9},{9,17},{17,25},{2,10},{10,18},{18,26},{... | collective-permute-start | bytes 49160 | tf_op jit(solution)/shard_map/ppermute | solution.py:19
  12.2 1.3 collective-permute-start.1
  13.5 0.9 slice_bitcast_fusion.8
  14.4 2.2 collective-permute-done.1
  16.7 0.8 pad_maximum_fusion.64
  17.5 11.1 %collective-permute-start.2 = (f32[4,1,18,128]{3,2,1,0:T(8,128)S(1)}, f32[4,1,18,128]{3,2,1,0:T(8,128)S(1)}, u32[]{:S(2)}, u32[]{:S(2)}) collective-permute-start(f32[4,1,18,128]{3,2,1,0:T(8,128)S(1)} %get-tuple-element.44), channel_id=1, source_target_pairs={{32,0},{64,32},{96,64},{128,96},{160,128},{192,160},{224,192},{256... | collective-permute-start | bytes 110600 | tf_op jit(solution)/shard_map/ppermute | solution.py:22
  28.6 1.9 collective-permute-start.3
  30.6 0.7 compare_select_fusion
  31.2 3.4 collective-permute-done.3
  34.7 1.0 pad_maximum_fusion
  35.9 3.5 collective-permute-start.4
  39.4 1.2 collective-permute-start.5
  40.6 1.6 subtract_multiply_fusion.5
  42.3 5.2 %collective-permute-done.4 = f32[4,10,18,1]{3,2,1,0:T(8,128)S(1)} collective-permute-done((f32[4,10,18,1]{3,2,1,0:T(8,128)S(1)}, f32[4,10,18,1]{3,2,1,0:T(8,128)S(1)}, u32[]{:S(2)}, u32[]{:S(2)}) %collective-permute-start.4) | collective-permute-done | bytes 2912 | tf_op jit(solution)/shard_map/ppermute | solution.py:22
  47.4 1.4 subtract_multiply_fusion.4
  48.9 1.4 fusion.24
  50.4 3.1 collective-permute-start.6
  53.5 1.3 collective-permute-start.7
  54.9 3.1 collective-permute-done.7
  58.0 1.9 collective-permute-start.8
  60.0 3.4 collective-permute-start.9
  63.4 2.6 collective-permute-done.9
  66.1 0.2 fusion.61
  66.3 4.2 %collective-permute-start.10 = (f32[4,10,18,1]{3,2,1,0:T(8,128)S(1)}, f32[4,10,18,1]{3,2,1,0:T(8,128)S(1)}, u32[]{:S(2)}, u32[]{:S(2)}) collective-permute-start(f32[4,10,18,1]{3,2,1,0:T(8,128)S(1)} %get-tuple-element.32), channel_id=1, source_target_pairs={{1,0},{2,1},{3,2},{4,3},{5,4},{6,5},{7,6},{0,7},{9,8},{10,9},{11,1... | collective-permute-start | bytes 8648 | tf_op jit(solution)/shard_map/ppermute | solution.py:22
  70.6 6.5 %collective-permute-done.10 = f32[4,10,18,1]{3,2,1,0:T(8,128)S(1)} collective-permute-done((f32[4,10,18,1]{3,2,1,0:T(8,128)S(1)}, f32[4,10,18,1]{3,2,1,0:T(8,128)S(1)}, u32[]{:S(2)}, u32[]{:S(2)}) %collective-permute-start.10) | collective-permute-done | bytes 2912 | tf_op jit(solution)/shard_map/ppermute | solution.py:22
  77.1 0.3 subtract_multiply_fusion.2
  77.8 2.8 collective-permute-start.12
  80.6 1.3 collective-permute-start.13
  82.0 3.2 collective-permute-done.13
  85.1 1.9 collective-permute-start.14
  87.1 3.5 collective-permute-start.15
  90.7 2.5 collective-permute-done.15
  93.4 5.4 %collective-permute-start.16 = (f32[4,10,18,1]{3,2,1,0:T(8,128)S(1)}, f32[4,10,18,1]{3,2,1,0:T(8,128)S(1)}, u32[]{:S(2)}, u32[]{:S(2)}) collective-permute-start(f32[4,10,18,1]{3,2,1,0:T(8,128)S(1)} %get-tuple-element.30), channel_id=1, source_target_pairs={{1,0},{2,1},{3,2},{4,3},{5,4},{6,5},{7,6},{0,7},{9,8},{10,9},{11,1... | collective-permute-start | bytes 8648 | tf_op jit(solution)/shard_map/ppermute | solution.py:22
  99.0 5.4 %collective-permute-done.16 = f32[4,10,18,1]{3,2,1,0:T(8,128)S(1)} collective-permute-done((f32[4,10,18,1]{3,2,1,0:T(8,128)S(1)}, f32[4,10,18,1]{3,2,1,0:T(8,128)S(1)}, u32[]{:S(2)}, u32[]{:S(2)}) %collective-permute-start.16) | collective-permute-done | bytes 2912 | tf_op jit(solution)/shard_map/ppermute | solution.py:22
  104.4 0.2 collective-permute-done.17
  104.6 0.3 subtract_multiply_fusion
  105.3 4.7 %copy.22 = f32[3,8,16,128]{0,3,2,1:T(8,128)} copy(f32[3,8,16,128]{3,2,1,0:T(8,128)S(1)} %slice.406) | data formatting | bytes 393216 | tf_op jit(solution)/shard_map/slice | solution.py:61
  110.0 4.1 %gather_fusion = f32[256,3]{1,0:T(8,128)S(1)} fusion(f32[3,16384]{0,1:T(8,128)} %bitcast.49, s32[1024]{0:T(1024)S(1)} %pad_clamp_fusion), kind=kCustom, calls=%fused_computation | custom fusion | bytes 7168 | tf_op jit(solution)/shard_map/jit(_take)/gather | solution.py:62
  114.2 1.1 convolution_bitcast_fusion
  115.9 231.1 %all-gather.3.cloned.1.call-done = f32[65536,128]{1,0:T(8,128)} async-done(((f32[128,128]{1,0:T(8,128)}), f32[65536,128]{1,0:T(8,128)}) %all-gather.3.cloned.1.call-update) | async-done | bytes 33554448 | tf_op jit(solution)/shard_map/all_gather | solution.py:67
  347.0 13.1 %reduce_sum.9 = f32[128,128]{1,0:T(8,128)S(1)} reduce(f32[512,128,128]{2,1,0:T(8,128)} %bitcast.48, f32[]{:T(128)} %constant.78.clone.1), dimensions={0}, to_apply=%region_0.1 | reduce | flops 8372224 | bytes 33619972 | tf_op jit(solution)/shard_map/reduce_sum | solution.py:67
  360.3 11.7 %cholesky.16 = f32[128,128]{1,0:T(8,128)S(1)} custom-call(f32[128,128]{1,0:T(8,128)S(1)} %fusion.57), custom_call_target="Cholesky" | custom-call | tf_op jit(solution)/shard_map/jit(cholesky)/cholesky | solution.py:68
  372.1 0.6 compare_reduce_fusion
  372.7 0.7 fusion.58
  373.4 9.8 %custom-call.7 = f32[1,128,128]{1,2,0:T(8,128)S(1)} custom-call(f32[1,128,128]{2,1,0:T(8,128)S(1)} %get-tuple-element.73), custom_call_target="InvertDiagBlocksLowerTriangular" | custom-call | tf_op jit(solution)/shard_map/jit(_solve_triangular)/triangular_solve | solution.py:69
  383.2 0.7 copy.29
  383.9 1.3 fusion.55
  (57 shorter events, 2.5 us)
Async XLA Ops:
  7.2 43.1 %copy-start = (f32[4,8,16,128]{3,2,1,0:T(8,128)S(1)}, f32[4,8,16,128]{3,2,1,0:T(8,128)}, u32[]{:S(2)}) copy-start(f32[4,8,16,128]{3,2,1,0:T(8,128)} %param.6) | copy-start | bytes 786436
  7.2 47.6 %copy-start.4 = (s32[256]{0:T(256)S(1)}, s32[256]{0:T(256)}, u32[]{:S(2)}) copy-start(s32[256]{0:T(256)} %param.8) | copy-start | bytes 3076
  7.2 339.8 %all-gather.3.cloned.1.call-start = ((), (), s32[]{:S(2)}) async-start(), calls=%async_computation | async-start | bytes 33619968 | tf_op jit(solution)/shard_map/all_gather | solution.py:67
  8.3 6.2 %collective-permute-start = (f32[4,8,1,128]{3,2,1,0:T(1,128)S(1)}, f32[4,8,1,128]{3,2,1,0:T(1,128)S(1)}, u32[]{:S(2)}, u32[]{:S(2)}) collective-permute-start(f32[4,8,1,128]{3,2,1,0:T(1,128)S(1)} %get-tuple-element.70), channel_id=1, source_target_pairs={{0,8},{8,16},{16,24},{1,9},{9,17},{17,25},{2,10},{10,18},{18,26},{... | collective-permute-start | bytes 49160 | tf_op jit(solution)/shard_map/ppermute | solution.py:19
  12.2 4.5 %collective-permute-start.1 = (f32[4,8,1,128]{3,2,1,0:T(1,128)S(1)}, f32[4,8,1,128]{3,2,1,0:T(1,128)S(1)}, u32[]{:S(2)}, u32[]{:S(2)}) collective-permute-start(f32[4,8,1,128]{3,2,1,0:T(1,128)S(1)} %get-tuple-element.71), channel_id=1, source_target_pairs={{8,0},{16,8},{24,16},{9,1},{17,9},{25,17},{10,2},{18,10},{26,18},{... | collective-permute-start | bytes 49160 | tf_op jit(solution)/shard_map/ppermute | solution.py:22
  17.5 13.7 %collective-permute-start.2 = (f32[4,1,18,128]{3,2,1,0:T(8,128)S(1)}, f32[4,1,18,128]{3,2,1,0:T(8,128)S(1)}, u32[]{:S(2)}, u32[]{:S(2)}) collective-permute-start(f32[4,1,18,128]{3,2,1,0:T(8,128)S(1)} %get-tuple-element.44), channel_id=1, source_target_pairs={{32,0},{64,32},{96,64},{128,96},{160,128},{192,160},{224,192},{256... | collective-permute-start | bytes 110600 | tf_op jit(solution)/shard_map/ppermute | solution.py:22
  28.6 6.0 %collective-permute-start.3 = (f32[4,1,18,128]{3,2,1,0:T(8,128)S(1)}, f32[4,1,18,128]{3,2,1,0:T(8,128)S(1)}, u32[]{:S(2)}, u32[]{:S(2)}) collective-permute-start(f32[4,1,18,128]{3,2,1,0:T(8,128)S(1)} %get-tuple-element.43), channel_id=1, source_target_pairs={{0,32},{32,64},{64,96},{96,128},{128,160},{160,192},{192,224},{224... | collective-permute-start | bytes 110600 | tf_op jit(solution)/shard_map/ppermute | solution.py:19
  35.7 41.8 %copy-start.3 = (f32[3]{0:T(128)S(1)}, f32[3]{0:T(128)}, u32[]{:S(2)}) copy-start(f32[3]{0:T(128)} %constant.81.clone) | copy-start | bytes 40
  35.9 11.5 %collective-permute-start.4 = (f32[4,10,18,1]{3,2,1,0:T(8,128)S(1)}, f32[4,10,18,1]{3,2,1,0:T(8,128)S(1)}, u32[]{:S(2)}, u32[]{:S(2)}) collective-permute-start(f32[4,10,18,1]{3,2,1,0:T(8,128)S(1)} %get-tuple-element.34), channel_id=1, source_target_pairs={{1,0},{2,1},{3,2},{4,3},{5,4},{6,5},{7,6},{0,7},{9,8},{10,9},{11,1... | collective-permute-start | bytes 8648 | tf_op jit(solution)/shard_map/ppermute | solution.py:22
  39.4 8.0 %collective-permute-start.5 = (f32[4,10,18,1]{3,2,1,0:T(8,128)S(1)}, f32[4,10,18,1]{3,2,1,0:T(8,128)S(1)}, u32[]{:S(2)}, u32[]{:S(2)}) collective-permute-start(f32[4,10,18,1]{3,2,1,0:T(8,128)S(1)} %get-tuple-element.35), channel_id=1, source_target_pairs={{0,1},{1,2},{2,3},{3,4},{4,5},{5,6},{6,7},{7,0},{8,9},{9,10},{10,1... | collective-permute-start | bytes 8648 | tf_op jit(solution)/shard_map/ppermute | solution.py:19
  50.4 4.5 %collective-permute-start.6 = (f32[4,8,1,128]{3,2,1,0:T(1,128)S(1)}, f32[4,8,1,128]{3,2,1,0:T(1,128)S(1)}, u32[]{:S(2)}, u32[]{:S(2)}) collective-permute-start(f32[4,8,1,128]{3,2,1,0:T(1,128)S(1)} %get-tuple-element.61), channel_id=1, source_target_pairs={{0,8},{8,16},{16,24},{1,9},{9,17},{17,25},{2,10},{10,18},{18,26},{... | collective-permute-start | bytes 49160 | tf_op jit(solution)/shard_map/ppermute | solution.py:19
  53.5 4.5 %collective-permute-start.7 = (f32[4,8,1,128]{3,2,1,0:T(1,128)S(1)}, f32[4,8,1,128]{3,2,1,0:T(1,128)S(1)}, u32[]{:S(2)}, u32[]{:S(2)}) collective-permute-start(f32[4,8,1,128]{3,2,1,0:T(1,128)S(1)} %get-tuple-element.62), channel_id=1, source_target_pairs={{8,0},{16,8},{24,16},{9,1},{17,9},{25,17},{10,2},{18,10},{26,18},{... | collective-permute-start | bytes 49160 | tf_op jit(solution)/shard_map/ppermute | solution.py:22
  58.0 5.3 %collective-permute-start.8 = (f32[4,1,18,128]{3,2,1,0:T(8,128)S(1)}, f32[4,1,18,128]{3,2,1,0:T(8,128)S(1)}, u32[]{:S(2)}, u32[]{:S(2)}) collective-permute-start(f32[4,1,18,128]{3,2,1,0:T(8,128)S(1)} %get-tuple-element.41), channel_id=1, source_target_pairs={{32,0},{64,32},{96,64},{128,96},{160,128},{192,160},{224,192},{256... | collective-permute-start | bytes 110600 | tf_op jit(solution)/shard_map/ppermute | solution.py:22
  60.0 6.0 %collective-permute-start.9 = (f32[4,1,18,128]{3,2,1,0:T(8,128)S(1)}, f32[4,1,18,128]{3,2,1,0:T(8,128)S(1)}, u32[]{:S(2)}, u32[]{:S(2)}) collective-permute-start(f32[4,1,18,128]{3,2,1,0:T(8,128)S(1)} %get-tuple-element.40), channel_id=1, source_target_pairs={{0,32},{32,64},{64,96},{96,128},{128,160},{160,192},{192,224},{224... | collective-permute-start | bytes 110600 | tf_op jit(solution)/shard_map/ppermute | solution.py:19
  66.3 10.9 %collective-permute-start.10 = (f32[4,10,18,1]{3,2,1,0:T(8,128)S(1)}, f32[4,10,18,1]{3,2,1,0:T(8,128)S(1)}, u32[]{:S(2)}, u32[]{:S(2)}) collective-permute-start(f32[4,10,18,1]{3,2,1,0:T(8,128)S(1)} %get-tuple-element.32), channel_id=1, source_target_pairs={{1,0},{2,1},{3,2},{4,3},{5,4},{6,5},{7,6},{0,7},{9,8},{10,9},{11,1... | collective-permute-start | bytes 8648 | tf_op jit(solution)/shard_map/ppermute | solution.py:22
  70.5 6.6 %collective-permute-start.11 = (f32[4,10,18,1]{3,2,1,0:T(8,128)S(1)}, f32[4,10,18,1]{3,2,1,0:T(8,128)S(1)}, u32[]{:S(2)}, u32[]{:S(2)}) collective-permute-start(f32[4,10,18,1]{3,2,1,0:T(8,128)S(1)} %get-tuple-element.33), channel_id=1, source_target_pairs={{0,1},{1,2},{2,3},{3,4},{4,5},{5,6},{6,7},{7,0},{8,9},{9,10},{10,1... | collective-permute-start | bytes 8648 | tf_op jit(solution)/shard_map/ppermute | solution.py:19
  77.8 4.2 %collective-permute-start.12 = (f32[4,8,1,128]{3,2,1,0:T(1,128)S(1)}, f32[4,8,1,128]{3,2,1,0:T(1,128)S(1)}, u32[]{:S(2)}, u32[]{:S(2)}) collective-permute-start(f32[4,8,1,128]{3,2,1,0:T(1,128)S(1)} %get-tuple-element.52), channel_id=1, source_target_pairs={{0,8},{8,16},{16,24},{1,9},{9,17},{17,25},{2,10},{10,18},{18,26},{... | collective-permute-start | bytes 49160 | tf_op jit(solution)/shard_map/ppermute | solution.py:19
  80.6 4.5 %collective-permute-start.13 = (f32[4,8,1,128]{3,2,1,0:T(1,128)S(1)}, f32[4,8,1,128]{3,2,1,0:T(1,128)S(1)}, u32[]{:S(2)}, u32[]{:S(2)}) collective-permute-start(f32[4,8,1,128]{3,2,1,0:T(1,128)S(1)} %get-tuple-element.53), channel_id=1, source_target_pairs={{8,0},{16,8},{24,16},{9,1},{17,9},{25,17},{10,2},{18,10},{26,18},{... | collective-permute-start | bytes 49160 | tf_op jit(solution)/shard_map/ppermute | solution.py:22
  85.1 5.5 %collective-permute-start.14 = (f32[4,1,18,128]{3,2,1,0:T(8,128)S(1)}, f32[4,1,18,128]{3,2,1,0:T(8,128)S(1)}, u32[]{:S(2)}, u32[]{:S(2)}) collective-permute-start(f32[4,1,18,128]{3,2,1,0:T(8,128)S(1)} %get-tuple-element.38), channel_id=1, source_target_pairs={{32,0},{64,32},{96,64},{128,96},{160,128},{192,160},{224,192},{256... | collective-permute-start | bytes 110600 | tf_op jit(solution)/shard_map/ppermute | solution.py:22
  87.1 6.0 %collective-permute-start.15 = (f32[4,1,18,128]{3,2,1,0:T(8,128)S(1)}, f32[4,1,18,128]{3,2,1,0:T(8,128)S(1)}, u32[]{:S(2)}, u32[]{:S(2)}) collective-permute-start(f32[4,1,18,128]{3,2,1,0:T(8,128)S(1)} %get-tuple-element.37), channel_id=1, source_target_pairs={{0,32},{32,64},{64,96},{96,128},{128,160},{160,192},{192,224},{224... | collective-permute-start | bytes 110600 | tf_op jit(solution)/shard_map/ppermute | solution.py:19
  93.4 11.0 %collective-permute-start.16 = (f32[4,10,18,1]{3,2,1,0:T(8,128)S(1)}, f32[4,10,18,1]{3,2,1,0:T(8,128)S(1)}, u32[]{:S(2)}, u32[]{:S(2)}) collective-permute-start(f32[4,10,18,1]{3,2,1,0:T(8,128)S(1)} %get-tuple-element.30), channel_id=1, source_target_pairs={{1,0},{2,1},{3,2},{4,3},{5,4},{6,5},{7,6},{0,7},{9,8},{10,9},{11,1... | collective-permute-start | bytes 8648 | tf_op jit(solution)/shard_map/ppermute | solution.py:22
  98.8 15.4 %copy-start.1 = (f32[127,3,256]{2,0,1:T(8,128)S(1)}, f32[127,3,256]{2,0,1:T(8,128)}, u32[]{:S(2)}) copy-start(f32[127,3,256]{2,0,1:T(8,128)} %param.7) | copy-start | bytes 1170436
  98.8 5.8 %collective-permute-start.17 = (f32[4,10,18,1]{3,2,1,0:T(8,128)S(1)}, f32[4,10,18,1]{3,2,1,0:T(8,128)S(1)}, u32[]{:S(2)}, u32[]{:S(2)}) collective-permute-start(f32[4,10,18,1]{3,2,1,0:T(8,128)S(1)} %get-tuple-element.31), channel_id=1, source_target_pairs={{0,1},{1,2},{2,3},{3,4},{4,5},{5,6},{6,7},{7,0},{8,9},{9,10},{10,1... | collective-permute-start | bytes 8648 | tf_op jit(solution)/shard_map/ppermute | solution.py:19
  105.2 254.8 %copy-start.2 = (f32[4,8,16,128]{3,2,1,0:T(8,128)}, f32[4,8,16,128]{3,2,1,0:T(8,128)S(1)}, u32[]{:S(2)}) copy-start(f32[4,8,16,128]{3,2,1,0:T(8,128)S(1)} %fusion.15) | copy-start | bytes 786436
Sparse Core Ops, SparseCore 0:
  115.5 231.4 all-gather.2
